TPU v7x, 32 devices: a whole 2x2x4 slice. The times are simulated.
32 devices in a mesh: vol: 8 (over z, x), nar: 4 (over y, core).
Axes of the slice: x: 2, y: 2, z: 4, core: 2. Of those that a mesh axis runs over, the one named last changes fastest.
Arguments:
- series: bfloat16 [2048, 2048], P(('vol', 'nar')), may hold values from -6 to 6
- send_rows: int32 [8, 4, 16], P('vol', 'nar'), may hold values from -1 to 63, as said below
- bin_counts: int32 [4], replicated, may hold values from 1 to 128, 256 in all
- observer_cells: int32 [2, 512], replicated, may hold values from 0 to 127
Outputs:
- spectra_out: float32 [4, 128, 2, 512], P('nar', 'vol')
Inputs may be any that keep to these rules, and one draw needn't show every extreme that they name: `send_rows`: entry (u, n, k) names the row of device (u, n)'s 64 rows of series for slot k mod 2 bound for the patch owner at vol index k // 2 and nar index n, or is -1 for an empty slot; one device never names a row twice. Nar index m owns bin_counts[m] bins in order, from the sum of the counts before m on; some owner holds exactly 128 bins. `observer_cells`: row 0 holds polar indices, row 1 azimuthal indices.
All inputs are finite; a program needn't handle non-finite values.
Results may differ from a plain program's by a relative error of at most 0.0043.
Values may be sent and summed in bfloat16 or wider, within the bound.
No kernel may reach another device: no remote copies, remote signals or barrier semaphores. Data moves between devices by JAX's collectives and lax.ppermute only.
A program may use at most 64 MiB of HBM per device.

v0:
```python
import math
import jax
import jax.numpy as jnp
from jax import lax
from jax.sharding import PartitionSpec as P

NF = 256
NQ = 4
WAVE_STEP = 0.05


def dft_table(bin_ids, keep_bin, time_len):
    time_steps = jnp.arange(time_len, dtype=jnp.int32)
    frequency = bin_ids + 1
    phase_turns = time_steps[:, None] * frequency[None, :] % time_len
    angle_grid = phase_turns.astype(jnp.float32) * (2.0 * math.pi / time_len)
    dft_grid = jnp.stack([jnp.cos(angle_grid), -jnp.sin(angle_grid)], axis=-1)
    dft_grid = jnp.where(keep_bin[None, :, None], dft_grid, jnp.float32(0.0))
    return dft_grid.reshape(time_len, 2 * bin_ids.shape[0]).astype(jnp.bfloat16)


def positions(point_list):
    beside_all = (point_list * 1597 % 8191).astype(jnp.float32) * (2.0 * math.pi / 8191.0)
    jitter = (point_list * 613 % 127).astype(jnp.float32) * (0.37 / 127.0)
    axial = (point_list // 128).astype(jnp.float32) * 0.5 + jitter
    return (20.0 * jnp.cos(beside_all), 20.0 * jnp.sin(beside_all), axial)


def directions(obs_cells):
    polar_angle = (obs_cells[0].astype(jnp.float32) + 0.5) * (math.pi / 128.0)
    azimuth = obs_cells[1].astype(jnp.float32) * (2.0 * math.pi / 128.0)
    return (
        jnp.sin(polar_angle) * jnp.cos(azimuth),
        jnp.sin(polar_angle) * jnp.sin(azimuth),
        jnp.cos(polar_angle),
    )


def project(facing, place_xyz):
    dotted = facing[0][:, None] * place_xyz[0][None, :] + facing[1][:, None] * place_xyz[1][None, :]
    return dotted + facing[2][:, None] * place_xyz[2][None, :]


def kernels(bin_ids, dotted):
    wavenumber = (bin_ids.astype(jnp.float32) + 1.0) * WAVE_STEP
    phase_grid = wavenumber[:, None, None] * dotted[None]
    return jnp.concatenate([jnp.cos(phase_grid), jnp.sin(phase_grid)], axis=1).astype(jnp.bfloat16)


def combine(products, bin_ids, facing, norm_scale):
    observers = facing[0].shape[0]
    bin_total = bin_ids.shape[0]
    cos_part = products[:, :observers].reshape(bin_total, observers, NQ, 2)
    sine_part = products[:, observers:].reshape(bin_total, observers, NQ, 2)
    real_part = cos_part[..., 0] + sine_part[..., 1]
    imag_part = cos_part[..., 1] - sine_part[..., 0]
    weights = jnp.stack([jnp.ones_like(facing[0]), facing[0], facing[1], facing[2]], axis=-1)
    real_sum = jnp.sum(real_part * weights[None], axis=-1)
    imag_sum = jnp.sum(imag_part * weights[None], axis=-1)
    amplitude = (bin_ids.astype(jnp.float32) + 1.0) * (norm_scale / NF)
    return jnp.stack([-amplitude[:, None] * imag_sum, amplitude[:, None] * real_sum], axis=1)


def apply_green(bin_ids, spec_block, dotted, facing, norm_scale):
    green_grid = kernels(bin_ids, dotted)
    products = jnp.einsum(
        "bxp,bcp->bxc", green_grid, spec_block, preferred_element_type=jnp.float32
    )
    return combine(products, bin_ids, facing, norm_scale)


def per_device(series, send_rows, bin_counts, observer_cells):
    vol_count = lax.axis_size("vol")
    nar_count = lax.axis_size("nar")
    vol_index = lax.axis_index("vol")
    nar_index = lax.axis_index("nar")
    bin_cap = vol_count * max(1, 2 * NF // (nar_count * vol_count))
    time_len = series.shape[1] // NQ
    slot_total = send_rows.shape[2]
    slot_width = slot_total // vol_count
    listing = send_rows.reshape(-1)
    picked = jnp.take(series, jnp.maximum(listing, 0), axis=0)
    packed = jnp.where((listing >= 0)[:, None], picked, jnp.zeros((), series.dtype))
    arrived = lax.all_to_all(packed, "vol", split_axis=0, concat_axis=0, tiled=True)
    starts = jnp.cumsum(bin_counts) - bin_counts
    own_start = starts[nar_index]
    own_count = bin_counts[nar_index]
    dft_scale = 1.0 / math.sqrt(time_len)
    within = jnp.arange(bin_cap, dtype=jnp.int32)
    own_table = dft_table(own_start + within, within < own_count, time_len)
    row_piece = lax.all_gather(arrived, "nar", axis=0, tiled=True)
    rows_here = row_piece.shape[0]
    spectral = jnp.dot(
        row_piece.reshape(rows_here * NQ, time_len), own_table, preferred_element_type=jnp.float32
    )
    spectral = (spectral * dft_scale).astype(jnp.bfloat16).reshape(rows_here, NQ, bin_cap, 2)
    spectra = spectral.transpose(2, 1, 3, 0).reshape(bin_cap, 2 * NQ, rows_here)
    local_points = nar_count * slot_total

    def point_ids(vol_owner, flat_index):
        nar_source = flat_index // slot_total
        remain = flat_index % slot_total
        vol_source = remain // slot_width
        within_slot = remain % slot_width
        return (
            (vol_source * nar_count + nar_source) * vol_count + vol_owner
        ) * slot_width + within_slot

    norm_scale = 1.0 / math.sqrt(vol_count * nar_count * slot_total)
    facing = directions(observer_cells)
    share_rows = bin_cap // vol_count
    regrouped = lax.all_to_all(spectra, "vol", split_axis=0, concat_axis=2, tiled=True)
    bin_ids = own_start + vol_index * share_rows + jnp.arange(share_rows, dtype=jnp.int32)
    span_points = local_points * max(1, vol_count // 8)
    turn_count = vol_count * local_points // span_points

    def add_block(turn_index, running):
        first_point = turn_index * span_points
        spec_block = lax.dynamic_slice_in_dim(regrouped, first_point, span_points, 2)
        flat_index = first_point + jnp.arange(span_points, dtype=jnp.int32)
        point_list = point_ids(flat_index // local_points, flat_index % local_points)
        dotted = project(facing, positions(point_list))
        return running + apply_green(bin_ids, spec_block, dotted, facing, norm_scale)

    result = lax.fori_loop(
        0, turn_count, add_block, jnp.zeros((share_rows, 2, observer_cells.shape[1]), jnp.float32)
    )
    return result.reshape(1, share_rows, 2, result.shape[-1])


def solution(mesh):
    placed = (P(("vol", "nar"), None), P("vol", "nar", None), P(), P())
    return jax.shard_map(
        per_device,
        mesh=mesh,
        in_specs=placed,
        out_specs=P("nar", "vol", None, None),
        check_vma=False,
    )
```

profile of v0, /device:TPU:0, one launch (start us, length us, event | category | flops | bytes accessed | tf_op | source)
XLA Modules:
  0.0 133.8 jit_solution(10418153351370994909)
XLA Ops:
  0.0 0.7 compare_reduce_fusion
  0.7 0.7 maximum_bitcast_fusion
  1.6 0.6 gather_fusion
  2.2 0.8 broadcast_select_fusion.1
  3.0 7.3 %all-to-all-start = ((bf16[8,2,2048]{2,1,0:T(2,128)(2,1)}), bf16[8,2,2048]{2,1,0:T(2,128)(2,1)S(1)}, u32[]{:S(2)}, u32[]{:S(2)}) async-start(bf16[8,2,2048]{2,1,0:T(2,128)(2,1)} %broadcast_select_fusion.1), calls=%async_computation | async-start | bytes 131072 | tf_op jit(solution)/shard_map/all_to_all | solution.py:84
  10.3 0.8 reduce-window.9
  11.1 0.7 bitcast_subtract_fusion
  11.8 1.3 dynamic_slice.18
  13.0 0.7 dynamic_slice.17
  13.7 0.7 add_add_fusion
  14.4 1.1 fusion.36
  15.5 0.6 iota_compare_fusion
  16.5 0.7 all-to-all-done
  17.2 5.8 %all_gather.3 = bf16[64,2048]{1,0:T(8,128)(2,1)S(1)} all-gather(bf16[16,2048]{1,0:T(8,128)(2,1)S(1)} %all_to_all.20), channel_id=1, replica_groups=mesh['vol'=8,'nar'=4] {'nar'}, dimensions={0}, use_global_device_ids=true | all-gather | bytes 327680 | tf_op jit(solution)/shard_map/all_gather | solution.py:91
  23.2 0.3 fusion.28
  23.5 10.0 %reshape.598 = bf16[64,4,128,2]{1,0,3,2:T(8,128)(2,1)} reshape(bf16[256,256]{0,1:T(8,128)(2,1)S(1)} %copy.27) | data formatting | bytes 262144 | tf_op jit(solution)/shard_map/reshape | solution.py:96
  33.5 6.2 %copy.28 = bf16[128,4,2,64]{0,3,2,1:T(8,128)(2,1)S(1)} copy(bf16[128,4,2,64]{1,3,2,0:T(8,128)(2,1)} %bitcast.64) | data formatting | bytes 262144 | tf_op jit(solution)/shard_map/transpose | solution.py:97
  39.9 0.9 reshape.631
  40.8 5.4 %all-to-all-start.1 = ((bf16[8,2,4096]{2,1,0:T(2,128)(2,1)}), bf16[8,2,4096]{2,1,0:T(2,128)(2,1)S(1)}, u32[]{:S(2)}, u32[]{:S(2)}) async-start(bf16[8,2,4096]{2,1,0:T(2,128)(2,1)} %reshape.631), calls=%async_computation.1 | async-start | bytes 262144 | tf_op jit(solution)/shard_map/all_to_all | solution.py:112
  47.0 6.6 %all-to-all-done.1 = bf16[8,2,4096]{2,1,0:T(2,128)(2,1)S(1)} async-done(((bf16[8,2,4096]{2,1,0:T(2,128)(2,1)}), bf16[8,2,4096]{2,1,0:T(2,128)(2,1)S(1)}, u32[]{:S(2)}, u32[]{:S(2)}) %all-to-all-start.1) | async-done | bytes 131104 | tf_op jit(solution)/shard_map/all_to_all | solution.py:112
  53.7 0.2 reshape.632
  54.1 0.2 all_to_all.24
  54.3 78.9 %while.19 = (s32[]{:T(128)}, f32[16,2,512]{2,1,0:T(2,128)S(1)}, f32[512]{0:T(512)S(1)}, f32[512]{0:T(512)S(1)}, f32[512]{0:T(512)S(1)}, /*index=5*/bf16[16,8,512...) while((s32[]{:T(128)}, f32[16,2,512]{2,1,0:T(2,128)S(1)}, ...), condition=%wide.region_4.5_spmd.clone.clone.clone, body=%wide.region_1.4_spmd.clone.clone.clone.sunk | while | flops 22971540 | bytes 8845429 | solution.py:125
  54.6 7.8 %fusion.56 = (bf16[16,512,64]{1,2,0:T(8,128)(2,1)S(1)}, bf16[16,512,64]{1,2,0:T(8,128)(2,1)S(1)}) fusion(f32[512,64]{0,1:T(8,128)S(1)} %multiply_add_fusion.2, f32[16]{0:T(128)S(1)} %fusion.55), kind=kLoop, calls=%fused_computation.5.clone.1 | loop fusion | flops 1572864 | bytes 2228288 | tf_op jit(solution)/shard_map/convert
  62.4 0.4 fusion.57
  63.2 0.3 slice_add_fusion.2
  64.5 7.8 %fusion.56 = (bf16[16,512,64]{1,2,0:T(8,128)(2,1)S(1)}, bf16[16,512,64]{1,2,0:T(8,128)(2,1)S(1)}) fusion(f32[512,64]{0,1:T(8,128)S(1)} %multiply_add_fusion.2, f32[16]{0:T(128)S(1)} %fusion.55), kind=kLoop, calls=%fused_computation.5.clone.1 | loop fusion | flops 1572864 | bytes 2228288 | tf_op jit(solution)/shard_map/convert
  72.2 0.4 fusion.57
  73.0 0.3 slice_add_fusion.2
  74.3 7.8 %fusion.56 = (bf16[16,512,64]{1,2,0:T(8,128)(2,1)S(1)}, bf16[16,512,64]{1,2,0:T(8,128)(2,1)S(1)}) fusion(f32[512,64]{0,1:T(8,128)S(1)} %multiply_add_fusion.2, f32[16]{0:T(128)S(1)} %fusion.55), kind=kLoop, calls=%fused_computation.5.clone.1 | loop fusion | flops 1572864 | bytes 2228288 | tf_op jit(solution)/shard_map/convert
  82.1 0.4 fusion.57
  82.9 0.3 slice_add_fusion.2
  84.2 7.8 %fusion.56 = (bf16[16,512,64]{1,2,0:T(8,128)(2,1)S(1)}, bf16[16,512,64]{1,2,0:T(8,128)(2,1)S(1)}) fusion(f32[512,64]{0,1:T(8,128)S(1)} %multiply_add_fusion.2, f32[16]{0:T(128)S(1)} %fusion.55), kind=kLoop, calls=%fused_computation.5.clone.1 | loop fusion | flops 1572864 | bytes 2228288 | tf_op jit(solution)/shard_map/convert
  92.0 0.4 fusion.57
  92.8 0.3 slice_add_fusion.2
  94.1 7.8 %fusion.56 = (bf16[16,512,64]{1,2,0:T(8,128)(2,1)S(1)}, bf16[16,512,64]{1,2,0:T(8,128)(2,1)S(1)}) fusion(f32[512,64]{0,1:T(8,128)S(1)} %multiply_add_fusion.2, f32[16]{0:T(128)S(1)} %fusion.55), kind=kLoop, calls=%fused_computation.5.clone.1 | loop fusion | flops 1572864 | bytes 2228288 | tf_op jit(solution)/shard_map/convert
  101.8 0.4 fusion.57
  102.6 0.3 slice_add_fusion.2
  103.9 7.8 %fusion.56 = (bf16[16,512,64]{1,2,0:T(8,128)(2,1)S(1)}, bf16[16,512,64]{1,2,0:T(8,128)(2,1)S(1)}) fusion(f32[512,64]{0,1:T(8,128)S(1)} %multiply_add_fusion.2, f32[16]{0:T(128)S(1)} %fusion.55), kind=kLoop, calls=%fused_computation.5.clone.1 | loop fusion | flops 1572864 | bytes 2228288 | tf_op jit(solution)/shard_map/convert
  111.7 0.4 fusion.57
  112.5 0.3 slice_add_fusion.2
  113.8 7.8 %fusion.56 = (bf16[16,512,64]{1,2,0:T(8,128)(2,1)S(1)}, bf16[16,512,64]{1,2,0:T(8,128)(2,1)S(1)}) fusion(f32[512,64]{0,1:T(8,128)S(1)} %multiply_add_fusion.2, f32[16]{0:T(128)S(1)} %fusion.55), kind=kLoop, calls=%fused_computation.5.clone.1 | loop fusion | flops 1572864 | bytes 2228288 | tf_op jit(solution)/shard_map/convert
  121.6 0.4 fusion.57
  122.4 0.3 slice_add_fusion.2
  123.6 7.8 %fusion.56 = (bf16[16,512,64]{1,2,0:T(8,128)(2,1)S(1)}, bf16[16,512,64]{1,2,0:T(8,128)(2,1)S(1)}) fusion(f32[512,64]{0,1:T(8,128)S(1)} %multiply_add_fusion.2, f32[16]{0:T(128)S(1)} %fusion.55), kind=kLoop, calls=%fused_computation.5.clone.1 | loop fusion | flops 1572864 | bytes 2228288 | tf_op jit(solution)/shard_map/convert
  131.4 0.4 fusion.57
  132.2 0.3 slice_add_fusion.2
  133.2 0.6 copy-done.1
  (139 shorter events, 11.0 us)
Async XLA Ops:
  0.0 1.6 %copy-start = (bf16[64,2048]{1,0:T(8,128)(2,1)S(1)}, bf16[64,2048]{1,0:T(8,128)(2,1)}, u32[]{:S(2)}) copy-start(bf16[64,2048]{1,0:T(8,128)(2,1)} %param.6) | copy-start | bytes 786436
  3.0 14.2 %all-to-all-start = ((bf16[8,2,2048]{2,1,0:T(2,128)(2,1)}), bf16[8,2,2048]{2,1,0:T(2,128)(2,1)S(1)}, u32[]{:S(2)}, u32[]{:S(2)}) async-start(bf16[8,2,2048]{2,1,0:T(2,128)(2,1)} %broadcast_select_fusion.1), calls=%async_computation | async-start | bytes 131072 | tf_op jit(solution)/shard_map/all_to_all | solution.py:84
  33.5 13.4 %copy-start.2 = (s32[2,512]{1,0:T(2,128)S(1)}, s32[2,512]{1,0:T(2,128)}, u32[]{:S(2)}) copy-start(s32[2,512]{1,0:T(2,128)} %param.9) | copy-start | bytes 12292
  40.8 12.9 %all-to-all-start.1 = ((bf16[8,2,4096]{2,1,0:T(2,128)(2,1)}), bf16[8,2,4096]{2,1,0:T(2,128)(2,1)S(1)}, u32[]{:S(2)}, u32[]{:S(2)}) async-start(bf16[8,2,4096]{2,1,0:T(2,128)(2,1)} %reshape.631), calls=%async_computation.1 | async-start | bytes 262144 | tf_op jit(solution)/shard_map/all_to_all | solution.py:112
  133.2 0.6 copy-start.1
where the time goes:
time: 134 us
  other arithmetic  78 us (58%)
  local copies, waits for them, and re-layouts  24.5 us (18%)
  starting transfers between devices  12.6 us (9%)
  waiting for transfers between devices  7.29 us (5%)
  blocking collectives  5.78 us (4%)
  matrix products  3.81 us (3%)
    another operation x9, other arithmetic  63 us
    reshape x1, local copies, waits for them, and re-layouts, per_device(): (spectral * dft_scale).astype(jnp.bfloat16)  9.98 us
    all_to_all x1, starting transfers between devices, per_device(): lax.all_to_all(packed, 'vol', split_axis=0, concat_axis=0, tiled=True)  7.28 us
    all_to_all x1, waiting for transfers between devices, per_device(): lax.all_to_all(spectra, 'vol', split_axis=0, concat_axis=2, tiled=True)  6.64 us
    transpose x1, local copies, waits for them, and re-layouts, per_device(): spectra = spectral.transpose(2, 1, 3, 0).reshape(bin_cap, 2 * NQ, rows_here)  6.2 us
    all_gather x1, blocking collectives, per_device(): row_piece = lax.all_gather(arrived, 'nar', axis=0, tiled=True)  5.78 us
    all_to_all x1, starting transfers between devices, per_device(): lax.all_to_all(spectra, 'vol', split_axis=0, concat_axis=2, tiled=True)  5.37 us
    dot_general x8, matrix products, apply_green(): jnp.einsum('bxp,bcp->bxc', green_grid, spec_block, preferred_element_type...  3.55 us
  transfers between devices with their start and end apart: 2, of which 2 were waited for; matrix products, arithmetic and copies ran while one was open for 5% of the time, Pallas kernels for 0%

commit v1 on v0

--- a/solution.py
+++ b/solution.py
@@ -7,6 +7,28 @@
 NF = 256
 NQ = 4
 WAVE_STEP = 0.05
+
+
+def in_blocks(array, dim, size):
+    before, after = (array.shape[:dim], array.shape[dim + 1 :])
+    return jnp.moveaxis(array.reshape(*before, size, -1, *after), dim, 0)
+
+
+def joined_along(pieces, dim):
+    pieces = jnp.moveaxis(pieces, 0, dim)
+    dims = pieces.shape
+    return pieces.reshape(*dims[:dim], dims[dim] * dims[dim + 1], *dims[dim + 2 :])
+
+
+def exchange_directly(x, axis, split_dim, concat_dim):
+    size, index = (lax.axis_size(axis), lax.axis_index(axis))
+    blocks = in_blocks(x, split_dim, size)
+    done = [blocks[index]]
+    for step in range(1, size):
+        sent = blocks[(index + step) % size]
+        done.append(lax.ppermute(sent, axis, [(i, (i + step) % size) for i in range(size)]))
+    blocks = jnp.stack(done)[(index - jnp.arange(size)) % size]
+    return joined_along(blocks, concat_dim)
 
 
 def dft_table(bin_ids, keep_bin, time_len):
@@ -81,7 +103,7 @@
     listing = send_rows.reshape(-1)
     picked = jnp.take(series, jnp.maximum(listing, 0), axis=0)
     packed = jnp.where((listing >= 0)[:, None], picked, jnp.zeros((), series.dtype))
-    arrived = lax.all_to_all(packed, "vol", split_axis=0, concat_axis=0, tiled=True)
+    arrived = exchange_directly(packed, "vol", 0, 0)
     starts = jnp.cumsum(bin_counts) - bin_counts
     own_start = starts[nar_index]
     own_count = bin_counts[nar_index]

time: 134 us -> 143 us (1.067)
  starting transfers between devices: 12.6 us -> 19.3 us
  waiting for transfers between devices: 7.29 us -> 8.85 us
    ppermute x0 -> x7, starting transfers between devices: none -> 13.9 us  [exchange_directly(): lax.ppermute(sent, axis, [(i, (i + step) % size) for i in range(size)])]
    all_to_all x1 -> x0, starting transfers between devices: 7.28 us -> none  [per_device(): lax.all_to_all(packed, 'vol', split_axis=0, concat_axis=0, tiled=True)]
    ppermute x0 -> x7, waiting for transfers between devices: none -> 2.11 us  [exchange_directly(): lax.ppermute(sent, axis, [(i, (i + step) % size) for i in range(size)])]
  transfers between devices with their start and end apart: 2 -> 8, of which waited for: 2 -> 3; matrix products, arithmetic and copies ran while one was open for 5% -> 4% of each run, Pallas kernels for 0% -> 0%
where the time goes in v1:
time: 143 us; the launch traced here: 142 us
  other arithmetic  77.3 us (54%)
  local copies, waits for them, and re-layouts  25.3 us (18%)
  starting transfers between devices  19.3 us (13%)
  waiting for transfers between devices  8.85 us (6%)
  blocking collectives  5.78 us (4%)
  matrix products  3.81 us (3%)
    another operation x9, other arithmetic  63 us
    ppermute x7, starting transfers between devices, exchange_directly(): lax.ppermute(sent, axis, [(i, (i + step) % size) for i in range(size)])  13.9 us
    reshape x1, local copies, waits for them, and re-layouts, per_device(): (spectral * dft_scale).astype(jnp.bfloat16)  9.98 us
    all_to_all x1, waiting for transfers between devices, per_device(): lax.all_to_all(spectra, 'vol', split_axis=0, concat_axis=2, tiled=True)  6.74 us
    transpose x1, local copies, waits for them, and re-layouts, per_device(): spectra = spectral.transpose(2, 1, 3, 0).reshape(bin_cap, 2 * NQ, rows_here)  6.2 us
    all_gather x1, blocking collectives, per_device(): row_piece = lax.all_gather(arrived, 'nar', axis=0, tiled=True)  5.78 us
    all_to_all x1, starting transfers between devices, per_device(): lax.all_to_all(spectra, 'vol', split_axis=0, concat_axis=2, tiled=True)  5.4 us
    dot_general x8, matrix products, apply_green(): jnp.einsum('bxp,bcp->bxc', green_grid, spec_block, preferred_element_type...  3.55 us
  transfers between devices with their start and end apart: 8, of which 3 were waited for; matrix products, arithmetic and copies ran while one was open for 4% of the time, Pallas kernels for 0%

profile of v1, /device:TPU:0, one launch (start us, length us, event | category | flops | bytes accessed | tf_op | source)
XLA Modules:
  0.0 142.2 jit_solution(1380495788933760546)
XLA Ops:
  0.0 0.7 compare_reduce_fusion
  0.7 0.7 maximum_bitcast_fusion
  1.6 0.6 gather_fusion
  2.5 3.0 %collective-permute-start = (bf16[2,2048]{1,0:T(2,128)(2,1)S(1)}, bf16[2,2048]{1,0:T(2,128)(2,1)S(1)}, u32[]{:S(2)}, u32[]{:S(2)}) collective-permute-start(bf16[2,2048]{1,0:T(2,128)(2,1)S(1)} %get-tuple-element.355), channel_id=1, source_target_pairs={{0,4},{4,8},{8,12},{12,16},{16,20},{20,24},{24,28},{28,0},{1,5},{5... | collective-permute-start | bytes 24584 | tf_op jit(solution)/shard_map/ppermute | solution.py:29
  5.5 1.6 %collective-permute-start.1 = (bf16[2,2048]{1,0:T(2,128)(2,1)S(1)}, bf16[2,2048]{1,0:T(2,128)(2,1)S(1)}, u32[]{:S(2)}, u32[]{:S(2)}) collective-permute-start(bf16[2,2048]{1,0:T(2,128)(2,1)S(1)} %get-tuple-element.354), channel_id=1, source_target_pairs={{0,8},{4,12},{8,16},{12,20},{16,24},{20,28},{24,0},{28,4},{1,9},{5... | collective-permute-start | bytes 24584 | tf_op jit(solution)/shard_map/ppermute | solution.py:29
  7.1 2.6 %collective-permute-start.2 = (bf16[2,2048]{1,0:T(2,128)(2,1)S(1)}, bf16[2,2048]{1,0:T(2,128)(2,1)S(1)}, u32[]{:S(2)}, u32[]{:S(2)}) collective-permute-start(bf16[2,2048]{1,0:T(2,128)(2,1)S(1)} %get-tuple-element.353), channel_id=1, source_target_pairs={{0,12},{4,16},{8,20},{12,24},{16,28},{20,0},{24,4},{28,8},{1,13},{... | collective-permute-start | bytes 24584 | tf_op jit(solution)/shard_map/ppermute | solution.py:29
  9.7 1.2 collective-permute-start.3
  10.9 2.6 %collective-permute-start.4 = (bf16[2,2048]{1,0:T(2,128)(2,1)S(1)}, bf16[2,2048]{1,0:T(2,128)(2,1)S(1)}, u32[]{:S(2)}, u32[]{:S(2)}) collective-permute-start(bf16[2,2048]{1,0:T(2,128)(2,1)S(1)} %get-tuple-element.351), channel_id=1, source_target_pairs={{0,20},{4,24},{8,28},{12,0},{16,4},{20,8},{24,12},{28,16},{1,21},{... | collective-permute-start | bytes 24584 | tf_op jit(solution)/shard_map/ppermute | solution.py:29
  13.5 0.8 reduce-window.9
  14.4 0.7 bitcast_subtract_fusion
  15.0 1.2 dynamic_slice.50
  16.2 0.6 dynamic_slice.41
  16.9 0.6 add_add_fusion
  17.5 1.1 fusion.36
  18.6 0.7 iota_compare_fusion
  19.7 1.4 collective-permute-start.5
  21.1 1.5 %collective-permute-start.6 = (bf16[2,2048]{1,0:T(2,128)(2,1)S(1)}, bf16[2,2048]{1,0:T(2,128)(2,1)S(1)}, u32[]{:S(2)}, u32[]{:S(2)}) collective-permute-start(bf16[2,2048]{1,0:T(2,128)(2,1)S(1)} %get-tuple-element.349), channel_id=1, source_target_pairs={{0,28},{4,0},{8,4},{12,8},{16,12},{20,16},{24,20},{28,24},{1,29},{... | collective-permute-start | bytes 24584 | tf_op jit(solution)/shard_map/ppermute | solution.py:29
  22.7 0.7 collective-permute-done.5
  23.4 1.4 collective-permute-done.6
  24.8 0.7 gather_fusion.1
  25.5 5.8 %all_gather.3 = bf16[64,2048]{1,0:T(8,128)(2,1)S(1)} all-gather(bf16[16,2048]{1,0:T(8,128)(2,1)S(1)} %reshape.648), channel_id=1, replica_groups=mesh['vol'=8,'nar'=4] {'nar'}, dimensions={0}, use_global_device_ids=true | all-gather | bytes 327680 | tf_op jit(solution)/shard_map/all_gather | solution.py:113
  31.8 10.0 %reshape.650 = bf16[64,4,128,2]{1,0,3,2:T(8,128)(2,1)} reshape(bf16[256,256]{0,1:T(8,128)(2,1)S(1)} %copy.27) | data formatting | bytes 262144 | tf_op jit(solution)/shard_map/reshape | solution.py:118
  41.8 6.2 %copy.28 = bf16[128,4,2,64]{0,3,2,1:T(8,128)(2,1)S(1)} copy(bf16[128,4,2,64]{1,3,2,0:T(8,128)(2,1)} %bitcast.94) | data formatting | bytes 262144 | tf_op jit(solution)/shard_map/transpose | solution.py:119
  48.2 0.9 reshape.691
  49.1 5.4 %all-to-all-start = ((bf16[8,2,4096]{2,1,0:T(2,128)(2,1)}), bf16[8,2,4096]{2,1,0:T(2,128)(2,1)S(1)}, u32[]{:S(2)}, u32[]{:S(2)}) async-start(bf16[8,2,4096]{2,1,0:T(2,128)(2,1)} %reshape.691), calls=%async_computation | async-start | bytes 262144 | tf_op jit(solution)/shard_map/all_to_all | solution.py:134
  55.3 6.7 %all-to-all-done = bf16[8,2,4096]{2,1,0:T(2,128)(2,1)S(1)} async-done(((bf16[8,2,4096]{2,1,0:T(2,128)(2,1)}), bf16[8,2,4096]{2,1,0:T(2,128)(2,1)S(1)}, u32[]{:S(2)}, u32[]{:S(2)}) %all-to-all-start) | async-done | bytes 131104 | tf_op jit(solution)/shard_map/all_to_all | solution.py:134
  62.6 78.9 %while.19 = (s32[]{:T(128)}, f32[16,2,512]{2,1,0:T(2,128)S(1)}, f32[512]{0:T(512)S(1)}, f32[512]{0:T(512)S(1)}, f32[512]{0:T(512)S(1)}, /*index=5*/bf16[16,8,512...) while((s32[]{:T(128)}, f32[16,2,512]{2,1,0:T(2,128)S(1)}, ...), condition=%wide.region_4.5_spmd.clone.clone.clone, body=%wide.region_1.4_spmd.clone.clone.clone.sunk | while | flops 22971540 | bytes 8845429 | solution.py:147
  63.0 7.8 %fusion.58 = (bf16[16,512,64]{1,2,0:T(8,128)(2,1)S(1)}, bf16[16,512,64]{1,2,0:T(8,128)(2,1)S(1)}) fusion(f32[512,64]{0,1:T(8,128)S(1)} %multiply_add_fusion.2, f32[16]{0:T(128)S(1)} %fusion.57), kind=kLoop, calls=%fused_computation.6.clone.1 | loop fusion | flops 1572864 | bytes 2228288 | tf_op jit(solution)/shard_map/convert
  70.8 0.4 fusion.59
  71.6 0.3 slice_add_fusion.2
  72.8 7.8 %fusion.58 = (bf16[16,512,64]{1,2,0:T(8,128)(2,1)S(1)}, bf16[16,512,64]{1,2,0:T(8,128)(2,1)S(1)}) fusion(f32[512,64]{0,1:T(8,128)S(1)} %multiply_add_fusion.2, f32[16]{0:T(128)S(1)} %fusion.57), kind=kLoop, calls=%fused_computation.6.clone.1 | loop fusion | flops 1572864 | bytes 2228288 | tf_op jit(solution)/shard_map/convert
  80.6 0.4 fusion.59
  82.7 7.8 %fusion.58 = (bf16[16,512,64]{1,2,0:T(8,128)(2,1)S(1)}, bf16[16,512,64]{1,2,0:T(8,128)(2,1)S(1)}) fusion(f32[512,64]{0,1:T(8,128)S(1)} %multiply_add_fusion.2, f32[16]{0:T(128)S(1)} %fusion.57), kind=kLoop, calls=%fused_computation.6.clone.1 | loop fusion | flops 1572864 | bytes 2228288 | tf_op jit(solution)/shard_map/convert
  90.5 0.4 fusion.59
  92.6 7.8 %fusion.58 = (bf16[16,512,64]{1,2,0:T(8,128)(2,1)S(1)}, bf16[16,512,64]{1,2,0:T(8,128)(2,1)S(1)}) fusion(f32[512,64]{0,1:T(8,128)S(1)} %multiply_add_fusion.2, f32[16]{0:T(128)S(1)} %fusion.57), kind=kLoop, calls=%fused_computation.6.clone.1 | loop fusion | flops 1572864 | bytes 2228288 | tf_op jit(solution)/shard_map/convert
  100.4 0.4 fusion.59
  101.2 0.3 slice_add_fusion.2
  102.4 7.8 %fusion.58 = (bf16[16,512,64]{1,2,0:T(8,128)(2,1)S(1)}, bf16[16,512,64]{1,2,0:T(8,128)(2,1)S(1)}) fusion(f32[512,64]{0,1:T(8,128)S(1)} %multiply_add_fusion.2, f32[16]{0:T(128)S(1)} %fusion.57), kind=kLoop, calls=%fused_computation.6.clone.1 | loop fusion | flops 1572864 | bytes 2228288 | tf_op jit(solution)/shard_map/convert
  110.2 0.4 fusion.59
  111.0 0.3 slice_add_fusion.2
  112.3 7.8 %fusion.58 = (bf16[16,512,64]{1,2,0:T(8,128)(2,1)S(1)}, bf16[16,512,64]{1,2,0:T(8,128)(2,1)S(1)}) fusion(f32[512,64]{0,1:T(8,128)S(1)} %multiply_add_fusion.2, f32[16]{0:T(128)S(1)} %fusion.57), kind=kLoop, calls=%fused_computation.6.clone.1 | loop fusion | flops 1572864 | bytes 2228288 | tf_op jit(solution)/shard_map/convert
  120.1 0.4 fusion.59
  122.2 7.8 %fusion.58 = (bf16[16,512,64]{1,2,0:T(8,128)(2,1)S(1)}, bf16[16,512,64]{1,2,0:T(8,128)(2,1)S(1)}) fusion(f32[512,64]{0,1:T(8,128)S(1)} %multiply_add_fusion.2, f32[16]{0:T(128)S(1)} %fusion.57), kind=kLoop, calls=%fused_computation.6.clone.1 | loop fusion | flops 1572864 | bytes 2228288 | tf_op jit(solution)/shard_map/convert
  130.0 0.4 fusion.59
  130.8 0.3 slice_add_fusion.2
  132.0 7.8 %fusion.58 = (bf16[16,512,64]{1,2,0:T(8,128)(2,1)S(1)}, bf16[16,512,64]{1,2,0:T(8,128)(2,1)S(1)}) fusion(f32[512,64]{0,1:T(8,128)S(1)} %multiply_add_fusion.2, f32[16]{0:T(128)S(1)} %fusion.57), kind=kLoop, calls=%fused_computation.6.clone.1 | loop fusion | flops 1572864 | bytes 2228288 | tf_op jit(solution)/shard_map/convert
  139.8 0.4 fusion.59
  141.6 0.6 copy-done.1
  (162 shorter events, 13.4 us)
Async XLA Ops:
  0.0 1.6 %copy-start = (bf16[64,2048]{1,0:T(8,128)(2,1)S(1)}, bf16[64,2048]{1,0:T(8,128)(2,1)}, u32[]{:S(2)}) copy-start(bf16[64,2048]{1,0:T(8,128)(2,1)} %param.6) | copy-start | bytes 786436
  2.5 17.2 %collective-permute-start = (bf16[2,2048]{1,0:T(2,128)(2,1)S(1)}, bf16[2,2048]{1,0:T(2,128)(2,1)S(1)}, u32[]{:S(2)}, u32[]{:S(2)}) collective-permute-start(bf16[2,2048]{1,0:T(2,128)(2,1)S(1)} %get-tuple-element.355), channel_id=1, source_target_pairs={{0,4},{4,8},{8,12},{12,16},{16,20},{20,24},{24,28},{28,0},{1,5},{5... | collective-permute-start | bytes 24584 | tf_op jit(solution)/shard_map/ppermute | solution.py:29
  5.5 15.6 %collective-permute-start.1 = (bf16[2,2048]{1,0:T(2,128)(2,1)S(1)}, bf16[2,2048]{1,0:T(2,128)(2,1)S(1)}, u32[]{:S(2)}, u32[]{:S(2)}) collective-permute-start(bf16[2,2048]{1,0:T(2,128)(2,1)S(1)} %get-tuple-element.354), channel_id=1, source_target_pairs={{0,8},{4,12},{8,16},{12,20},{16,24},{20,28},{24,0},{28,4},{1,9},{5... | collective-permute-start | bytes 24584 | tf_op jit(solution)/shard_map/ppermute | solution.py:29
  7.1 15.5 %collective-permute-start.2 = (bf16[2,2048]{1,0:T(2,128)(2,1)S(1)}, bf16[2,2048]{1,0:T(2,128)(2,1)S(1)}, u32[]{:S(2)}, u32[]{:S(2)}) collective-permute-start(bf16[2,2048]{1,0:T(2,128)(2,1)S(1)} %get-tuple-element.353), channel_id=1, source_target_pairs={{0,12},{4,16},{8,20},{12,24},{16,28},{20,0},{24,4},{28,8},{1,13},{... | collective-permute-start | bytes 24584 | tf_op jit(solution)/shard_map/ppermute | solution.py:29
  9.7 13.0 %collective-permute-start.3 = (bf16[2,2048]{1,0:T(2,128)(2,1)S(1)}, bf16[2,2048]{1,0:T(2,128)(2,1)S(1)}, u32[]{:S(2)}, u32[]{:S(2)}) collective-permute-start(bf16[2,2048]{1,0:T(2,128)(2,1)S(1)} %get-tuple-element.352), channel_id=1, source_target_pairs={{0,16},{4,20},{8,24},{12,28},{16,0},{20,4},{24,8},{28,12},{1,17},{... | collective-permute-start | bytes 24584 | tf_op jit(solution)/shard_map/ppermute | solution.py:29
  10.9 11.8 %collective-permute-start.4 = (bf16[2,2048]{1,0:T(2,128)(2,1)S(1)}, bf16[2,2048]{1,0:T(2,128)(2,1)S(1)}, u32[]{:S(2)}, u32[]{:S(2)}) collective-permute-start(bf16[2,2048]{1,0:T(2,128)(2,1)S(1)} %get-tuple-element.351), channel_id=1, source_target_pairs={{0,20},{4,24},{8,28},{12,0},{16,4},{20,8},{24,12},{28,16},{1,21},{... | collective-permute-start | bytes 24584 | tf_op jit(solution)/shard_map/ppermute | solution.py:29
  19.7 3.7 %collective-permute-start.5 = (bf16[2,2048]{1,0:T(2,128)(2,1)S(1)}, bf16[2,2048]{1,0:T(2,128)(2,1)S(1)}, u32[]{:S(2)}, u32[]{:S(2)}) collective-permute-start(bf16[2,2048]{1,0:T(2,128)(2,1)S(1)} %get-tuple-element.350), channel_id=1, source_target_pairs={{0,24},{4,28},{8,0},{12,4},{16,8},{20,12},{24,16},{28,20},{1,25},{... | collective-permute-start | bytes 24584 | tf_op jit(solution)/shard_map/ppermute | solution.py:29
  21.1 3.7 %collective-permute-start.6 = (bf16[2,2048]{1,0:T(2,128)(2,1)S(1)}, bf16[2,2048]{1,0:T(2,128)(2,1)S(1)}, u32[]{:S(2)}, u32[]{:S(2)}) collective-permute-start(bf16[2,2048]{1,0:T(2,128)(2,1)S(1)} %get-tuple-element.349), channel_id=1, source_target_pairs={{0,28},{4,0},{8,4},{12,8},{16,12},{20,16},{24,20},{28,24},{1,29},{... | collective-permute-start | bytes 24584 | tf_op jit(solution)/shard_map/ppermute | solution.py:29
  41.8 13.3 %copy-start.2 = (s32[2,512]{1,0:T(2,128)S(1)}, s32[2,512]{1,0:T(2,128)}, u32[]{:S(2)}) copy-start(s32[2,512]{1,0:T(2,128)} %param.9) | copy-start | bytes 12292
  49.1 12.9 %all-to-all-start = ((bf16[8,2,4096]{2,1,0:T(2,128)(2,1)}), bf16[8,2,4096]{2,1,0:T(2,128)(2,1)S(1)}, u32[]{:S(2)}, u32[]{:S(2)}) async-start(bf16[8,2,4096]{2,1,0:T(2,128)(2,1)} %reshape.691), calls=%async_computation | async-start | bytes 262144 | tf_op jit(solution)/shard_map/all_to_all | solution.py:134
  141.6 0.6 copy-start.1
